TPU v7x, 32 devices: a whole 2x2x4 slice. The times are simulated.
32 devices in a mesh: col: 4 (over y, x), bulk: 8 (over z, core).
Axes of the slice: x: 2, y: 2, z: 4, core: 2. Of those that a mesh axis runs over, the one named last changes fastest.
Arguments:
- sequence_embedding: bfloat16 [64, 128, 64], P('bulk', 'col'), may hold values from -6 to 6
- residue_couplings: bfloat16 [128, 128, 128], P('bulk', 'col'), may hold values from -6 to 6
- sequence_layernorm_factor: float32 [64], replicated, may hold values from 0.5 to 1.5
- coupling_layernorm_factor: float32 [128], replicated, may hold values from 0.5 to 1.5
- content_projection: bfloat16 [64, 256], replicated, may hold values from -0.75 to 0.75
- switch_projection: bfloat16 [64, 256], replicated, may hold values from -0.75 to 0.75
- attention_score_projection: bfloat16 [128, 8], replicated, may hold values from -0.29882812 to 0.29882812
- final_projection: bfloat16 [256, 64], replicated, may hold values from -2 to 2
- residual_change_cotangent: bfloat16 [64, 128, 64], P('bulk', 'col'), may hold values from -6 to 6
Outputs:
- residual_change: bfloat16 [64, 128, 64], P('bulk', 'col')
- sequence_embedding_sensitivity: bfloat16 [64, 128, 64], P('bulk', 'col')
- coupling_sensitivity: bfloat16 [128, 128, 128], P('bulk', 'col')
All inputs are finite; a program needn't handle non-finite values.
Results may differ from a plain program's by a relative error of at most 0.025.
Values may be sent and summed in bfloat16 or wider, within the bound.
A program may use at most 64 MiB of HBM per device.

v0:
```python
import jax
import jax.numpy as jnp
from jax import lax
from jax.sharding import PartitionSpec as P

epsilon = 1e-05


def centred_sequences(inputs, scale_gain):
    widened = inputs.astype(jnp.float32)
    row_mean = jnp.mean(widened, axis=-1, keepdims=True)
    centered = widened - row_mean
    variance = jnp.mean(centered * centered, axis=-1, keepdims=True)
    inv_std = lax.rsqrt(variance + epsilon)
    normed = centered * inv_std
    return (normed * scale_gain, normed, inv_std)


def layernorm_reverse_mode(upstream, normed, inv_std, scale_gain):
    scaled = upstream * scale_gain
    mean_grad = jnp.mean(scaled, axis=-1, keepdims=True)
    mean_proj = jnp.mean(scaled * normed, axis=-1, keepdims=True)
    return inv_std * (scaled - mean_grad - normed * mean_proj)


def per_device(
    sequence_embedding,
    residue_couplings,
    sequence_layernorm_factor,
    coupling_layernorm_factor,
    content_projection,
    switch_projection,
    attention_score_projection,
    final_projection,
    residual_change_cotangent,
):
    number_of_heads = attention_score_projection.shape[1]
    value_channels = content_projection.shape[1]
    head_channels = value_channels // number_of_heads
    device_sequences = sequence_embedding.shape[0]
    device_residues = sequence_embedding.shape[1]
    finest_accuracy = lax.Precision.HIGHEST
    out_wide = final_projection.astype(jnp.float32)
    switch_single_form = switch_projection.astype(jnp.float32)
    bias_wide = attention_score_projection.astype(jnp.float32)
    pair_scaled, pair_hat, pair_inv = centred_sequences(
        residue_couplings, coupling_layernorm_factor
    )
    logits = jnp.einsum(
        "ijk,kh->hij",
        pair_scaled.astype(jnp.bfloat16),
        attention_score_projection,
        preferred_element_type=jnp.float32,
    )
    exponent = jnp.exp(logits)
    totals = lax.psum(jnp.sum(exponent, axis=2), "col")
    weights = exponent / totals[:, :, None]
    weights_low = weights.astype(jnp.bfloat16)
    weight_panel = lax.all_gather(weights_low, "bulk", axis=1, tiled=True)
    all_tokens = weight_panel.shape[1]
    sequence_scaled_by_factor, sequence_centred_unit, sequence_reciprocal_spread = (
        centred_sequences(sequence_embedding, sequence_layernorm_factor)
    )
    sequence_embedding_brief = sequence_scaled_by_factor.astype(jnp.bfloat16)
    content_sequences = jnp.dot(
        sequence_embedding_brief, content_projection, preferred_element_type=jnp.float32
    ).astype(jnp.bfloat16)
    value_per_head = content_sequences.reshape(
        device_sequences, device_residues, number_of_heads, head_channels
    )
    partial_value = jnp.einsum(
        "hij,sjhc->sihc", weight_panel, value_per_head, preferred_element_type=jnp.float32
    ).reshape(device_sequences, all_tokens, value_channels)
    partial_low = partial_value.astype(jnp.bfloat16)
    sigmoid_switch = jax.nn.sigmoid(
        jnp.dot(sequence_embedding_brief, switch_projection, preferred_element_type=jnp.float32)
    )
    pair_average = lax.psum_scatter(partial_low, "col", scatter_dimension=1, tiled=True).astype(
        jnp.float32
    )
    residual_change = jnp.dot(
        sigmoid_switch * pair_average, out_wide, precision=finest_accuracy
    ).astype(jnp.bfloat16)
    d_gated = jnp.dot(
        residual_change_cotangent.astype(jnp.float32), out_wide.T, precision=finest_accuracy
    )
    d_average_here = (sigmoid_switch * d_gated).astype(jnp.bfloat16)
    average_gradient = lax.all_gather(d_average_here, "col", axis=1, tiled=True)
    switch_preimage_sensitivity = d_gated * pair_average * sigmoid_switch * (1.0 - sigmoid_switch)
    gate_contribution = jnp.dot(
        switch_preimage_sensitivity, switch_single_form.T, precision=finest_accuracy
    )
    head_gradient = average_gradient.reshape(
        device_sequences, all_tokens, number_of_heads, head_channels
    )
    content_sensitivity = jnp.einsum(
        "hij,sihc->sjhc", weight_panel, head_gradient, preferred_element_type=jnp.float32
    )
    content_sensitivity = content_sensitivity.reshape(
        device_sequences, device_residues, value_channels
    ).astype(jnp.bfloat16)
    weight_part = jnp.einsum(
        "sihc,sjhc->hij", head_gradient, value_per_head, preferred_element_type=jnp.float32
    )
    d_weights = lax.psum_scatter(
        weight_part.astype(jnp.bfloat16), "bulk", scatter_dimension=1, tiled=True
    ).astype(jnp.float32)
    row_dot = lax.psum(jnp.sum(weights_low.astype(jnp.float32) * d_weights, axis=2), "col")
    d_logits = weights * (d_weights - row_dot[:, :, None])
    d_pair_low = jnp.einsum("hij,kh->ijk", d_logits, bias_wide, precision=finest_accuracy)
    coupling_sensitivity = layernorm_reverse_mode(
        d_pair_low, pair_hat, pair_inv, coupling_layernorm_factor
    ).astype(jnp.bfloat16)
    sequence_sensitivity_brief = (
        jnp.dot(content_sensitivity, content_projection.T, preferred_element_type=jnp.float32)
        + gate_contribution
    )
    sequence_embedding_sensitivity = layernorm_reverse_mode(
        sequence_sensitivity_brief,
        sequence_centred_unit,
        sequence_reciprocal_spread,
        sequence_layernorm_factor,
    ).astype(jnp.bfloat16)
    return (residual_change, sequence_embedding_sensitivity, coupling_sensitivity)


def solution(mesh):
    in_specs = (
        P("bulk", "col", None),
        P("bulk", "col", None),
        P(),
        P(),
        P(),
        P(),
        P(),
        P(),
        P("bulk", "col", None),
    )
    out_specs = (P("bulk", "col", None), P("bulk", "col", None), P("bulk", "col", None))
    return jax.shard_map(
        per_device, mesh=mesh, in_specs=in_specs, out_specs=out_specs, check_vma=False
    )
```

profile of v0, /device:TPU:0, one launch (start us, length us, event | category | flops | bytes accessed | tf_op | source)
XLA Modules:
  0.0 105.6 jit_solution(678878752773036502)
XLA Ops:
  7.2 0.0 copy-start
  7.2 0.0 reduce-scatter.5.cloned.1.call-start
  7.2 1.0 convert_reduce_fusion.1
  8.2 0.0 copy-done.1
  8.2 0.0 copy-start.4
  8.2 0.2 fusion.39
  8.4 0.0 copy-start.8
  8.5 0.5 copy-done.4
  9.0 0.1 copy-done.8
  9.1 0.2 convolution_convert_fusion.2
  9.4 0.0 copy-start.5
  9.4 0.2 reshape.60
  9.6 0.5 copy-done.5
  10.1 0.2 fusion.50
  10.3 0.6 copy-done.6
  10.9 0.3 multiply_convert_fusion
  11.2 11.5 %all_gather.7 = bf16[8,128,256]{2,1,0:T(8,128)(2,1)S(1)} all-gather(bf16[8,32,256]{2,1,0:T(8,128)(2,1)S(1)} %get-tuple-element.9), channel_id=1, replica_groups=mesh['col'=4,'bulk'=8] {'col'}, dimensions={1}, use_global_device_ids=true | all-gather | bytes 655360 | tf_op jit(solution)/shard_map/all_gather | solution.py:88
  22.7 0.3 copy.58
  23.0 0.3 fusion.6
  23.3 0.9 copy.64
  24.2 0.0 reduce-scatter.5.cloned.1.call-update
  24.2 0.0 reduce-scatter.3.cloned.1.call-start
  24.3 0.8 copy-done.2
  25.1 0.1 convert_reduce_fusion
  25.2 0.3 fusion.21
  25.5 0.0 copy-start.9
  25.5 0.0 copy-start.10
  25.5 0.6 copy-done.9
  26.2 0.4 fusion.65
  26.6 9.1 %psum.14 = f32[8,16]{0,1:T(8,128)S(1)} all-reduce(f32[8,16]{0,1:T(8,128)S(1)} %get-tuple-element.11), channel_id=1, replica_groups=mesh['col'=4,'bulk'=8] {'col'}, use_global_device_ids=true, to_apply=%region_5.0 | all-reduce | flops 128 | bytes 1024 | tf_op jit(solution)/shard_map/psum | solution.py:56
  35.7 19.7 %reduce-scatter.5.cloned.1.call-done = bf16[8,16,32]{2,0,1:T(8,128)(2,1)} async-done(((bf16[8,128,32]{2,0,1:T(8,128)(2,1)}), bf16[8,16,32]{2,0,1:T(8,128)(2,1)}) %reduce-scatter.5.cloned.1.call-update) | async-done | bytes 8208 | tf_op jit(solution)/shard_map/reduce_scatter | solution.py:105
  55.4 0.9 fusion.45
  56.3 14.2 %all_gather.6 = bf16[8,128,32]{2,0,1:T(8,128)(2,1)S(1)} all-gather(bf16[8,16,32]{2,0,1:T(8,128)(2,1)S(1)} %get-tuple-element.8), channel_id=1, replica_groups=mesh['col'=4,'bulk'=8] {'bulk'}, dimensions={1}, use_global_device_ids=true | all-gather | bytes 73728 | tf_op jit(solution)/shard_map/all_gather | solution.py:59
  70.5 0.4 fusion
  70.9 1.0 copy.57
  71.9 0.0 reduce-scatter.3.cloned.1.call-update
  71.9 0.3 fusion.1
  72.2 0.3 copy.61
  72.6 0.4 convert_element_type.78
  73.0 10.5 %psum.15 = f32[8,16]{0,1:T(8,128)S(1)} all-reduce(f32[8,16]{0,1:T(8,128)S(1)} %get-tuple-element.7), channel_id=1, replica_groups=mesh['col'=4,'bulk'=8] {'col'}, use_global_device_ids=true, to_apply=%region_11.0 | all-reduce | flops 128 | bytes 1024 | tf_op jit(solution)/shard_map/psum | solution.py:108
  83.4 0.7 fusion.62
  84.1 1.0 fusion.20
  85.1 10.4 %reduce-scatter.3.cloned.1.call-done = bf16[8,32,256]{2,1,0:T(8,128)(2,1)} async-done(((bf16[8,128,256]{2,1,0:T(8,128)(2,1)}), bf16[8,32,256]{2,1,0:T(8,128)(2,1)}) %reduce-scatter.3.cloned.1.call-update) | async-done | bytes 131088 | tf_op jit(solution)/shard_map/reduce_scatter | solution.py:78
  95.5 1.2 %fusion.24 = f32[8,32,64]{2,1,0:T(8,128)S(1)} fusion(f32[8,32,256]{2,1,0:T(8,128)S(1)} %get-tuple-element.10, f32[8,32,256]{2,1,0:T(8,128)S(1)} %fusion.50, bf16[8,32,256]{2,1,0:T(8,128)(2,1)} %reduce-scatter.3.cloned.1.call-done, bf16[64,256]{1,0:T(8,128)(2,1)S(1)} %copy-done.6), kind=kOutput, calls=%fused_computation.37 | convolution fusion | flops 50659328 | bytes 753664 | tf_op jit(solution)/shard_map/dot_general | solution.py:90
  96.7 0.3 fusion.63
  97.0 0.8 fusion.38
  97.9 0.1 copy-done.3
  97.9 0.9 convolution_convert_fusion.3
  (15 shorter events, 0.1 us)
Async XLA Ops:
  7.2 2.4 %copy-start = (bf16[8,32,64]{2,1,0:T(8,128)(2,1)S(1)}, bf16[8,32,64]{2,1,0:T(8,128)(2,1)}, u32[]{:S(2)}) copy-start(bf16[8,32,64]{2,1,0:T(8,128)(2,1)} %param.17) | copy-start | bytes 98308
  7.2 1.0 copy-start.1
  7.2 48.2 %reduce-scatter.5.cloned.1.call-start = ((), (), s32[]{:S(2)}) async-start(), calls=%async_computation.3 | async-start | bytes 294912 | tf_op jit(solution)/shard_map/reduce_scatter | solution.py:105
  8.2 0.8 copy-start.4
  8.4 0.7 copy-start.8
  9.4 0.8 copy-start.5
  10.1 0.8 copy-start.6
  24.2 0.9 copy-start.2
  24.2 71.3 %reduce-scatter.3.cloned.1.call-start = ((), (), s32[]{:S(2)}) async-start(), calls=%async_computation.2 | async-start | bytes 655360 | tf_op jit(solution)/shard_map/reduce_scatter | solution.py:78
  25.5 0.7 copy-start.9
  25.5 0.7 copy-start.10
  72.6 10.8 %copy-start.7 = (bf16[8,16,32]{2,0,1:T(8,128)(2,1)S(1)}, bf16[8,16,32]{2,0,1:T(8,128)(2,1)}, u32[]{:S(2)}) copy-start(bf16[8,16,32]{2,0,1:T(8,128)(2,1)} %reduce-scatter.5.cloned.1.call-done) | copy-start | bytes 24580
  97.0 0.9 copy-start.3
Sparse Core Ops, SparseCore 0:
  24.3 31.0 reduce-scatter.4
  72.1 23.4 reduce-scatter.2
where the time goes:
time: 106 us
  blocking collectives  45.3 us (43%)
  waiting for transfers between devices  30.1 us (28%)
  between operations  14.3 us (13%)
  local copies, waits for them, and re-layouts  6.44 us (6%)
  matrix products  5.12 us (5%)
  other arithmetic  4.33 us (4%)
    reduce_scatter x1, waiting for transfers between devices, per_device(): lax.psum_scatter(weight_part.astype(jnp.bfloat16), 'bulk', scatter_dimens...  19.7 us
    all_gather x1, blocking collectives, per_device(): weight_panel = lax.all_gather(weights_low, 'bulk', axis=1, tiled=True)  14.2 us
    all_gather x1, blocking collectives, per_device(): average_gradient = lax.all_gather(d_average_here, 'col', axis=1, tiled=True)  11.5 us
    psum x1, blocking collectives, per_device(): lax.psum(jnp.sum(weights_low.astype(jnp.float32) * d_weights, axis=2), 'c...  10.5 us
    reduce_scatter x1, waiting for transfers between devices, per_device(): lax.psum_scatter(partial_low, 'col', scatter_dimension=1, tiled=True)  10.4 us
    psum x1, blocking collectives, per_device(): totals = lax.psum(jnp.sum(exponent, axis=2), 'col')  9.09 us
    unnamed x22, local copies, waits for them, and re-layouts  3.31 us
  transfers between devices with their start and end apart: 2, of which 2 were waited for; matrix products, arithmetic and copies ran while one was open for 3% of the time, Pallas kernels for 0%

commit v1 on v0

--- a/solution.py
+++ b/solution.py
@@ -85,7 +85,12 @@
         residual_change_cotangent.astype(jnp.float32), out_wide.T, precision=finest_accuracy
     )
     d_average_here = (sigmoid_switch * d_gated).astype(jnp.bfloat16)
-    average_gradient = lax.all_gather(d_average_here, "col", axis=1, tiled=True)
+    ring = [d_average_here]
+    for hop in range(3):
+        ring.append(lax.ppermute(ring[-1], "col", [(dev, (dev + 1) % 4) for dev in range(4)]))
+    average_gradient = jnp.roll(
+        jnp.concatenate(ring[::-1], axis=1), (lax.axis_index("col") + 1) * ring[0].shape[1], axis=1
+    )
     switch_preimage_sensitivity = d_gated * pair_average * sigmoid_switch * (1.0 - sigmoid_switch)
     gate_contribution = jnp.dot(
         switch_preimage_sensitivity, switch_single_form.T, precision=finest_accuracy

time: 106 us -> 113 us (1.066)
  waiting for transfers between devices: 30.1 us -> 47.4 us
  blocking collectives: 45.3 us -> 32.4 us
  starting transfers between devices: 0.08 us -> 3.89 us
  local copies, waits for them, and re-layouts: 6.44 us -> 5.09 us
    ppermute x0 -> x3, waiting for transfers between devices: none -> 14.5 us  [per_device(): lax.ppermute(ring[-1], 'col', [(dev, (dev + 1) % 4) for dev in range(4)])]
    all_gather x1 -> x0, blocking collectives: 11.5 us -> none  [per_device(): average_gradient = lax.all_gather(d_average_here, 'col', axis=1, tiled=True)]
    ppermute x0 -> x3, starting transfers between devices: none -> 3.81 us  [per_device(): lax.ppermute(ring[-1], 'col', [(dev, (dev + 1) % 4) for dev in range(4)])]
    reduce_scatter x1, waiting for transfers between devices: 19.7 us -> 22.5 us  [per_device(): lax.psum_scatter(weight_part.astype(jnp.bfloat16), 'bulk', scatter_dimens...]
    unnamed x22 -> x29, local copies, waits for them, and re-layouts: 3.31 us -> 1.91 us
    psum x1, blocking collectives: 9.09 us -> 7.85 us  [per_device(): totals = lax.psum(jnp.sum(exponent, axis=2), 'col')]
  transfers between devices with their start and end apart: 2 -> 5, of which waited for: 2 -> 5; matrix products, arithmetic and copies ran while one was open for 3% -> 4% of each run, Pallas kernels for 0% -> 0%
where the time goes in v1:
time: 113 us
  waiting for transfers between devices  47.4 us (42%)
  blocking collectives  32.4 us (29%)
  between operations  14.4 us (13%)
  matrix products  5.14 us (5%)
  local copies, waits for them, and re-layouts  5.09 us (5%)
  other arithmetic  4.33 us (4%)
  starting transfers between devices  3.89 us (3%)
    reduce_scatter x1, waiting for transfers between devices, per_device(): lax.psum_scatter(weight_part.astype(jnp.bfloat16), 'bulk', scatter_dimens...  22.5 us
    ppermute x3, waiting for transfers between devices, per_device(): lax.ppermute(ring[-1], 'col', [(dev, (dev + 1) % 4) for dev in range(4)])  14.5 us
    all_gather x1, blocking collectives, per_device(): weight_panel = lax.all_gather(weights_low, 'bulk', axis=1, tiled=True)  14.2 us
    reduce_scatter x1, waiting for transfers between devices, per_device(): lax.psum_scatter(partial_low, 'col', scatter_dimension=1, tiled=True)  10.4 us
    psum x1, blocking collectives, per_device(): lax.psum(jnp.sum(weights_low.astype(jnp.float32) * d_weights, axis=2), 'c...  10.4 us
    psum x1, blocking collectives, per_device(): totals = lax.psum(jnp.sum(exponent, axis=2), 'col')  7.85 us
    ppermute x3, starting transfers between devices, per_device(): lax.ppermute(ring[-1], 'col', [(dev, (dev + 1) % 4) for dev in range(4)])  3.81 us
  transfers between devices with their start and end apart: 5, of which 5 were waited for; matrix products, arithmetic and copies ran while one was open for 4% of the time, Pallas kernels for 0%

profile of v1, /device:TPU:0, one launch (start us, length us, event | category | flops | bytes accessed | tf_op | source)
XLA Modules:
  0.0 112.6 jit_solution(13685824485507282666)
XLA Ops:
  7.2 0.0 copy-start
  7.2 0.0 copy-start.1
  7.2 0.0 reduce-scatter.5.cloned.1.call-start
  7.2 1.0 convert_reduce_fusion.1
  8.2 0.0 copy-start.5
  8.2 0.2 fusion.39
  8.4 0.0 copy-done
  8.5 0.5 copy-done.5
  9.0 0.2 fusion.50
  9.2 0.6 copy-done.6
  9.8 0.3 multiply_convert_fusion
  10.0 0.0 copy-start.2
  10.1 3.0 %collective-permute-start = (bf16[8,32,256]{2,1,0:T(8,128)(2,1)S(1)}, bf16[8,32,256]{2,1,0:T(8,128)(2,1)S(1)}, u32[]{:S(2)}, u32[]{:S(2)}) collective-permute-start(bf16[8,32,256]{2,1,0:T(8,128)(2,1)S(1)} %get-tuple-element.9), channel_id=1, source_target_pairs={{0,8},{8,16},{16,24},{24,0},{1,9},{9,17},{17,25},{25,1},{2,10},{10... | collective-permute-start | bytes 393224 | tf_op jit(solution)/shard_map/ppermute | solution.py:90
  13.1 0.3 convolution_convert_fusion.2
  13.3 0.1 convert_reduce_fusion
  13.5 4.0 %collective-permute-done = bf16[8,32,256]{2,1,0:T(8,128)(2,1)S(1)} collective-permute-done((bf16[8,32,256]{2,1,0:T(8,128)(2,1)S(1)}, bf16[8,32,256]{2,1,0:T(8,128)(2,1)S(1)}, u32[]{:S(2)}, u32[]{:S(2)}) %collective-permute-start) | collective-permute-done | bytes 131104 | tf_op jit(solution)/shard_map/ppermute | solution.py:90
  17.5 0.8 collective-permute-start.1
  18.3 0.2 reshape.60
  18.6 0.3 fusion.21
  18.8 4.6 %collective-permute-done.1 = bf16[8,32,256]{2,1,0:T(8,128)(2,1)S(1)} collective-permute-done((bf16[8,32,256]{2,1,0:T(8,128)(2,1)S(1)}, bf16[8,32,256]{2,1,0:T(8,128)(2,1)S(1)}, u32[]{:S(2)}, u32[]{:S(2)}) %collective-permute-start.1) | collective-permute-done | bytes 131104 | tf_op jit(solution)/shard_map/ppermute | solution.py:90
  23.4 0.0 collective-permute-start.2
  23.4 5.9 %collective-permute-done.2 = bf16[8,32,256]{2,1,0:T(8,128)(2,1)S(1)} collective-permute-done((bf16[8,32,256]{2,1,0:T(8,128)(2,1)S(1)}, bf16[8,32,256]{2,1,0:T(8,128)(2,1)S(1)}, u32[]{:S(2)}, u32[]{:S(2)}) %collective-permute-start.2) | collective-permute-done | bytes 131104 | tf_op jit(solution)/shard_map/ppermute | solution.py:90
  29.5 0.3 copy.56
  29.7 0.3 fusion.6
  30.1 0.9 copy.62
  31.0 0.0 reduce-scatter.5.cloned.1.call-update
  31.0 0.0 reduce-scatter.3.cloned.1.call-start
  31.0 0.6 copy-done.9
  31.6 0.4 fusion.65
  32.1 7.9 %psum.14 = f32[8,16]{0,1:T(8,128)S(1)} all-reduce(f32[8,16]{0,1:T(8,128)S(1)} %get-tuple-element.11), channel_id=1, replica_groups=mesh['col'=4,'bulk'=8] {'col'}, use_global_device_ids=true, to_apply=%region_5.0 | all-reduce | flops 128 | bytes 1024 | tf_op jit(solution)/shard_map/psum | solution.py:56
  39.9 22.5 %reduce-scatter.5.cloned.1.call-done = bf16[8,16,32]{2,0,1:T(8,128)(2,1)} async-done(((bf16[8,128,32]{2,0,1:T(8,128)(2,1)}), bf16[8,16,32]{2,0,1:T(8,128)(2,1)}) %reduce-scatter.5.cloned.1.call-update) | async-done | bytes 8208 | tf_op jit(solution)/shard_map/reduce_scatter | solution.py:110
  62.4 0.9 fusion.45
  63.4 14.2 %all_gather.3 = bf16[8,128,32]{2,0,1:T(8,128)(2,1)S(1)} all-gather(bf16[8,16,32]{2,0,1:T(8,128)(2,1)S(1)} %get-tuple-element.8), channel_id=1, replica_groups=mesh['col'=4,'bulk'=8] {'bulk'}, dimensions={1}, use_global_device_ids=true | all-gather | bytes 73728 | tf_op jit(solution)/shard_map/all_gather | solution.py:59
  77.6 0.4 fusion
  78.0 1.0 copy.55
  79.0 0.0 reduce-scatter.3.cloned.1.call-update
  79.0 0.3 fusion.1
  79.3 0.3 copy.59
  79.7 0.4 convert_element_type.78
  80.0 10.4 %psum.15 = f32[8,16]{0,1:T(8,128)S(1)} all-reduce(f32[8,16]{0,1:T(8,128)S(1)} %get-tuple-element.7), channel_id=1, replica_groups=mesh['col'=4,'bulk'=8] {'col'}, use_global_device_ids=true, to_apply=%region_11.12 | all-reduce | flops 128 | bytes 1024 | tf_op jit(solution)/shard_map/psum | solution.py:113
  90.4 0.7 fusion.62
  91.1 1.0 fusion.20
  92.1 10.4 %reduce-scatter.3.cloned.1.call-done = bf16[8,32,256]{2,1,0:T(8,128)(2,1)} async-done(((bf16[8,128,256]{2,1,0:T(8,128)(2,1)}), bf16[8,32,256]{2,1,0:T(8,128)(2,1)}) %reduce-scatter.3.cloned.1.call-update) | async-done | bytes 131088 | tf_op jit(solution)/shard_map/reduce_scatter | solution.py:78
  102.5 1.2 %fusion.24 = f32[8,32,64]{2,1,0:T(8,128)S(1)} fusion(f32[8,32,256]{2,1,0:T(8,128)S(1)} %get-tuple-element.10, f32[8,32,256]{2,1,0:T(8,128)S(1)} %fusion.50, bf16[8,32,256]{2,1,0:T(8,128)(2,1)} %reduce-scatter.3.cloned.1.call-done, bf16[64,256]{1,0:T(8,128)(2,1)S(1)} %copy-done.6), kind=kOutput, calls=%fused_computation.37 | convolution fusion | flops 50659328 | bytes 753664 | tf_op jit(solution)/shard_map/dot_general | solution.py:95
  103.7 0.3 fusion.63
  104.0 0.8 fusion.38
  104.8 0.1 copy-done.3
  104.9 0.9 convolution_convert_fusion.3
  (29 shorter events, 0.2 us)
Async XLA Ops:
  7.2 1.3 %copy-start = (bf16[8,32,64]{2,1,0:T(8,128)(2,1)S(1)}, bf16[8,32,64]{2,1,0:T(8,128)(2,1)}, u32[]{:S(2)}) copy-start(bf16[8,32,64]{2,1,0:T(8,128)(2,1)} %param.17) | copy-start | bytes 98308
  7.2 1.0 copy-start.1
  7.2 55.3 %reduce-scatter.5.cloned.1.call-start = ((), (), s32[]{:S(2)}) async-start(), calls=%async_computation.3 | async-start | bytes 294912 | tf_op jit(solution)/shard_map/reduce_scatter | solution.py:110
  8.2 0.8 copy-start.5
  9.0 0.8 copy-start.6
  9.0 0.8 copy-start.8
  9.8 3.3 %copy-start.4 = (bf16[64,256]{1,0:T(8,128)(2,1)S(1)}, bf16[64,256]{1,0:T(8,128)(2,1)}, u32[]{:S(2)}) copy-start(bf16[64,256]{1,0:T(8,128)(2,1)} %param.13) | copy-start | bytes 98308
  10.0 3.3 %copy-start.2 = (bf16[16,32,128]{2,1,0:T(8,128)(2,1)S(1)}, bf16[16,32,128]{2,1,0:T(8,128)(2,1)}, u32[]{:S(2)}) copy-start(bf16[16,32,128]{2,1,0:T(8,128)(2,1)} %param.10) | copy-start | bytes 393220
  10.1 7.5 %collective-permute-start = (bf16[8,32,256]{2,1,0:T(8,128)(2,1)S(1)}, bf16[8,32,256]{2,1,0:T(8,128)(2,1)S(1)}, u32[]{:S(2)}, u32[]{:S(2)}) collective-permute-start(bf16[8,32,256]{2,1,0:T(8,128)(2,1)S(1)} %get-tuple-element.9), channel_id=1, source_target_pairs={{0,8},{8,16},{16,24},{24,0},{1,9},{9,17},{17,25},{25,1},{2,10},{10... | collective-permute-start | bytes 393224 | tf_op jit(solution)/shard_map/ppermute | solution.py:90
  17.5 5.9 %collective-permute-start.1 = (bf16[8,32,256]{2,1,0:T(8,128)(2,1)S(1)}, bf16[8,32,256]{2,1,0:T(8,128)(2,1)S(1)}, u32[]{:S(2)}, u32[]{:S(2)}) collective-permute-start(bf16[8,32,256]{2,1,0:T(8,128)(2,1)S(1)} %collective-permute-done), channel_id=1, source_target_pairs={{0,8},{8,16},{16,24},{24,0},{1,9},{9,17},{17,25},{25,1},{2,10},{10... | collective-permute-start | bytes 393224 | tf_op jit(solution)/shard_map/ppermute | solution.py:90
  23.4 5.9 %collective-permute-start.2 = (bf16[8,32,256]{2,1,0:T(8,128)(2,1)S(1)}, bf16[8,32,256]{2,1,0:T(8,128)(2,1)S(1)}, u32[]{:S(2)}, u32[]{:S(2)}) collective-permute-start(bf16[8,32,256]{2,1,0:T(8,128)(2,1)S(1)} %collective-permute-done.1), channel_id=1, source_target_pairs={{0,8},{8,16},{16,24},{24,0},{1,9},{9,17},{17,25},{25,1},{2,10},{10... | collective-permute-start | bytes 393224 | tf_op jit(solution)/shard_map/ppermute | solution.py:90
  31.0 0.7 copy-start.9
  31.0 0.7 copy-start.10
  31.0 71.5 %reduce-scatter.3.cloned.1.call-start = ((), (), s32[]{:S(2)}) async-start(), calls=%async_computation.2 | async-start | bytes 655360 | tf_op jit(solution)/shard_map/reduce_scatter | solution.py:78
  79.6 10.8 %copy-start.7 = (bf16[8,16,32]{2,0,1:T(8,128)(2,1)S(1)}, bf16[8,16,32]{2,0,1:T(8,128)(2,1)}, u32[]{:S(2)}) copy-start(bf16[8,16,32]{2,0,1:T(8,128)(2,1)} %reduce-scatter.5.cloned.1.call-done) | copy-start | bytes 24580
  104.0 0.9 copy-start.3
Sparse Core Ops, SparseCore 0:
  31.1 31.2 reduce-scatter.4
  79.1 23.3 reduce-scatter.2
